TPU v7x, 256 devices: a whole 4x4x8 slice. The times are simulated.
256 devices in a mesh: attn: 32 (over y, z), proj: 8 (over x, core).
Axes of the slice: x: 4, y: 4, z: 8, core: 2. Of those that a mesh axis runs over, the one named last changes fastest.
Arguments:
- tokens: bfloat16 [16384, 4096], P('attn', 'proj'), may hold values from -6 to 6
- norm_gain: float32 [4096], replicated, may hold values from 0.1 to 1.9
- w_query: bfloat16 [4096, 4096], P(None, 'proj')
- w_key: bfloat16 [4096, 1024], P(None, 'proj')
- value_matrix: bfloat16 [4096, 1024], P(None, 'proj'), may hold values from -0.09375 to 0.09375
- doc_lengths: int32 [128], replicated, may hold values from 1 to 512, 16384 in all
- block_server: int32 [128], P('attn'), may hold values from 0 to 31, as said below
Outputs:
- attn_out: bfloat16 [16384, 4096], P('attn', 'proj')
- served_lse: float32 [128, 32, 128], P('attn', 'proj')
Inputs may be any that keep to these rules, and one draw needn't show every extreme that they name: `doc_lengths`: the lengths sum to 16384. `block_server`: query block b belongs to the micro-batch b // 4; every index of attn serves exactly 4 blocks, and at most one block of any one micro-batch.
All inputs are finite; a program needn't handle non-finite values.
Results may differ from a plain program's by a relative error of at most 0.0074.
Values may be sent and summed in bfloat16 or wider, within the bound.
A program may use at most 128 MiB of HBM per device.

v0:
```python
import jax
import jax.numpy as jnp
from jax import lax
from jax.sharding import PartitionSpec as P

HEAD = 128
QB = 128
NEG = -1e30
norm_eps = 1e-05


def shards(tokens, norm_gain, w_query, w_key, value_matrix, doc_lengths, block_server):
    rows = tokens.shape[0]
    model_width = w_query.shape[0]
    heads = w_query.shape[1] // HEAD
    blocks = rows // QB
    servers = lax.axis_size("attn")
    me = lax.axis_index("attn")
    wide = lax.all_gather(tokens, "proj", axis=1, tiled=True).astype(jnp.float32)
    scaled = (wide * norm_gain[None, :]).astype(jnp.bfloat16)
    squares = jnp.sum(wide * wide, axis=1, keepdims=True)
    inverse = lax.rsqrt(squares / model_width + norm_eps)
    dot = lambda w: (jnp.dot(scaled, w, preferred_element_type=jnp.float32) * inverse).astype(
        jnp.bfloat16
    )
    k = dot(w_key)
    v = dot(value_matrix)
    kv = jnp.concatenate([k, v], axis=1)
    prior = lax.ppermute(kv, "attn", [(i, (i + 1) % servers) for i in range(servers)])
    q = dot(w_query)
    allkv = jnp.concatenate([prior, kv], axis=0)
    starts = jnp.cumsum(doc_lengths) - doc_lengths
    extent = rows + QB
    outs, lses = ([], [])
    for b in range(blocks):
        pos = me * rows + b * QB + jnp.arange(QB, dtype=jnp.int32)
        first = jnp.max(jnp.where(starts[None, :] <= pos[:, None], starts[None, :], 0), axis=1)
        kpos = (me - 1) * rows + b * QB + jnp.arange(extent, dtype=jnp.int32)
        allowed = (kpos[None, :] >= first[:, None]) & (kpos[None, :] <= pos[:, None])
        win = allkv[b * QB : b * QB + extent]
        qb = q[b * QB : (b + 1) * QB].reshape(QB, heads, HEAD)
        s = jnp.einsum("qhd,kd->hqk", qb, win[:, :HEAD], preferred_element_type=jnp.float32)
        s = jnp.where(allowed, s * (1.0 / HEAD**0.5), NEG)
        m = jnp.max(s, axis=-1)
        w = jnp.where(allowed, jnp.exp(s - m[..., None]), 0.0)
        total = jnp.sum(w, axis=-1)
        o = jnp.einsum(
            "hqk,kd->hqd", w.astype(jnp.bfloat16), win[:, HEAD:], preferred_element_type=jnp.float32
        )
        o = (o / total[..., None]).transpose(1, 0, 2).reshape(QB, heads * HEAD).astype(jnp.bfloat16)
        outs.append(o)
        lses.append(m + jnp.log(total))
    attn_out = jnp.concatenate(outs, axis=0)
    lse = jnp.stack(lses)
    slot = jnp.arange(servers, dtype=jnp.int32)
    sending = block_server[None, :] == slot[:, None]
    send = jnp.sum(jnp.where(sending[:, :, None, None], lse[None], 0.0), axis=1)
    flag = jnp.any(sending, axis=1).astype(jnp.float32)
    send = jnp.concatenate([send, jnp.broadcast_to(flag[:, None, None], (servers, 1, QB))], axis=1)
    recv = lax.all_to_all(send, "attn", split_axis=0, concat_axis=0, tiled=True)
    valid = recv[:, heads, 0] > 0
    rank = jnp.cumsum(valid.astype(jnp.int32)) - 1
    pick = (rank[None, :] == jnp.arange(blocks, dtype=jnp.int32)[:, None]) & valid[None, :]
    served = jnp.sum(jnp.where(pick[:, :, None, None], recv[None, :, :heads], 0.0), axis=1)
    return (attn_out, served)


def solution(mesh):
    return jax.shard_map(
        shards,
        mesh=mesh,
        in_specs=(
            P("attn", "proj"),
            P(),
            P(None, "proj"),
            P(None, "proj"),
            P(None, "proj"),
            P(),
            P("attn"),
        ),
        out_specs=(P("attn", "proj"), P("attn", "proj", None)),
        check_vma=False,
    )
```

profile of v0, /device:TPU:32, one launch (start us, length us, event | category | flops | bytes accessed | tf_op | source)
XLA Modules:
  0.0 96.2 jit_solution(9389079406854169225)
XLA Ops:
  7.2 0.7 all-gather.2.cloned.1.call-update
  7.9 0.7 iota_compare_fusion.1
  8.7 0.8 copy.85
  9.7 0.7 sub.48
  11.2 35.8 %all-gather.2.cloned.1.call-done = bf16[512,4096]{1,0:T(8,128)(2,1)} async-done(((bf16[512,512]{1,0:T(8,128)(2,1)}), bf16[512,4096]{1,0:T(8,128)(2,1)}) %all-gather.2.cloned.1.call-update) | async-done | bytes 4194320 | tf_op jit(solution)/shard_map/all_gather | solution.py:19
  47.0 3.2 %fusion.1 = f32[512]{0:T(512)S(1)} fusion(bf16[512,4096]{1,0:T(8,128)(2,1)} %all-gather.2.cloned.1.call-done), kind=kLoop, calls=%fused_computation.3 | loop fusion | flops 6290944 | bytes 4196352 | tf_op jit(solution)/shard_map/reduce_sum | solution.py:21
  50.5 1.5 %fusion.36 = bf16[512,128]{0,1:T(8,128)(2,1)S(1)} fusion(bf16[4096,128]{1,0:T(8,128)(2,1)S(1)} %copy-done, bf16[512,4096]{1,0:T(8,128)(2,1)S(1)} %copy-done.1, f32[4096]{0:T(1024)S(1)} %copy-done.4, f32[512]{0:T(512)S(1)} %add_rsqrt_fusion), kind=kOutput, calls=%fused_computation.39 | convolution fusion | flops 543293440 | bytes 5392384 | tf_op jit(solution)/shard_map/dot_general | solution.py:23
  52.0 1.5 %fusion.39 = bf16[512,128]{0,1:T(8,128)(2,1)S(1)} fusion(bf16[4096,128]{1,0:T(8,128)(2,1)S(1)} %copy-done.3, bf16[512,4096]{1,0:T(8,128)(2,1)S(1)} %copy-done.1, f32[4096]{0:T(1024)S(1)} %copy-done.4, f32[512]{0:T(512)S(1)} %add_rsqrt_fusion), kind=kOutput, calls=%fused_computation.40 | convolution fusion | flops 543293440 | bytes 5392384 | tf_op jit(solution)/shard_map/dot_general | solution.py:23
  53.6 1.6 %collective-permute-start = (bf16[512,256]{0,1:T(8,128)(2,1)S(1)}, bf16[512,256]{0,1:T(8,128)(2,1)S(1)}, u32[]{:S(2)}, u32[]{:S(2)}) collective-permute-start(bf16[512,256]{0,1:T(8,128)(2,1)S(1)} %pad_maximum_fusion.1), channel_id=1, source_target_pairs={{0,8},{8,16},{16,24},{24,32},{32,40},{40,48},{48,56},{56,64},{64,7... | collective-permute-start | bytes 786440 | tf_op jit(solution)/shard_map/ppermute | solution.py:29
  55.2 2.4 %fusion.19 = bf16[512,512]{0,1:T(8,128)(2,1)S(1)} fusion(bf16[4096,512]{1,0:T(8,128)(2,1)S(1)} %copy-done.2, bf16[512,4096]{1,0:T(8,128)(2,1)S(1)} %copy-done.1, f32[4096]{0:T(1024)S(1)} %copy-done.4, f32[512]{0:T(512)S(1)} %add_rsqrt_fusion), kind=kOutput, calls=%fused_computation.24 | convolution fusion | flops 2154299392 | bytes 8931328 | tf_op jit(solution)/shard_map/dot_general | solution.py:23
  57.8 4.4 %collective-permute-done = bf16[512,256]{0,1:T(8,128)(2,1)S(1)} collective-permute-done((bf16[512,256]{0,1:T(8,128)(2,1)S(1)}, bf16[512,256]{0,1:T(8,128)(2,1)S(1)}, u32[]{:S(2)}, u32[]{:S(2)}) %collective-permute-start) | collective-permute-done | bytes 262176 | tf_op jit(solution)/shard_map/ppermute | solution.py:29
  62.2 0.4 fusion.73
  63.2 0.4 fusion.74
  63.9 0.4 fusion.34
  64.2 0.4 fusion.75
  65.2 0.4 fusion.76
  66.1 0.7 copy.102
  66.8 11.3 %all-to-all-start = ((f32[32,5,128]{2,1,0:T(8,128)}), f32[32,5,128]{2,1,0:T(8,128)S(1)}, u32[]{:S(2)}, u32[]{:S(2)}) async-start(f32[32,5,128]{2,1,0:T(8,128)} %copy.102), calls=%async_computation | async-start | bytes 262144 | tf_op jit(solution)/shard_map/all_to_all | solution.py:60
  78.1 1.0 %fusion.32 = bf16[128,4,128]{0,2,1:T(8,128)(2,1)} fusion(f32[4,128,640]{1,2,0:T(8,128)S(1)} %get-tuple-element.21, f32[4,128]{1,0:T(4,128)S(1)} %get-tuple-element.20, pred[128,640]{0,1:T(8,128)(4,1)S(1)} %get-tuple-element.25, bf16[1024,256]{0,1:T(8,128)(2,1)S(1)} %maximum_maximum_fusion, f32[128,4]{0,1:T(4,128)S(1)} %bitcast.110), kind=kOutput, calls=%fused_computation.35 | convolution fusion | flops 85000192 | bytes 1691648 | tf_op jit(solution)/shard_map/hqk,kd->hqd/dot_general | solution.py:47
  79.4 1.0 %copy.98 = bf16[128,512]{1,0:T(8,128)(2,1)S(1)} copy(bf16[128,512]{0,1:T(8,128)(2,1)} %bitcast.104) | data formatting | bytes 262144 | tf_op jit(solution)/shard_map/convert_element_type | solution.py:50
  80.4 0.8 pad_maximum_fusion
  81.3 6.4 %all-to-all-done = f32[32,5,128]{2,1,0:T(8,128)S(1)} async-done(((f32[32,5,128]{2,1,0:T(8,128)}), f32[32,5,128]{2,1,0:T(8,128)S(1)}, u32[]{:S(2)}, u32[]{:S(2)}) %all-to-all-start) | async-done | bytes 81952 | tf_op jit(solution)/shard_map/all_to_all | solution.py:60
  87.8 0.7 compare_reduce_fusion
  88.6 0.7 select_reduce_fusion
  (51 shorter events, 3.9 us)
Async XLA Ops:
  7.2 43.1 %copy-start = (bf16[4096,128]{1,0:T(8,128)(2,1)S(1)}, bf16[4096,128]{1,0:T(8,128)(2,1)}, u32[]{:S(2)}) copy-start(bf16[4096,128]{1,0:T(8,128)(2,1)} %param.11) | copy-start | bytes 3145732
  7.2 39.9 %all-gather.2.cloned.1.call-start = ((), (), s32[]{:S(2)}) async-start(), calls=%async_computation.1 | async-start | bytes 4718592 | tf_op jit(solution)/shard_map/all_gather | solution.py:19
  11.0 39.3 %copy-start.4 = (f32[4096]{0:T(1024)S(1)}, f32[4096]{0:T(1024)}, u32[]{:S(2)}) copy-start(f32[4096]{0:T(1024)} %param.8) | copy-start | bytes 49156
  47.0 3.4 %copy-start.1 = (bf16[512,4096]{1,0:T(8,128)(2,1)S(1)}, bf16[512,4096]{1,0:T(8,128)(2,1)}, u32[]{:S(2)}) copy-start(bf16[512,4096]{1,0:T(8,128)(2,1)} %all-gather.2.cloned.1.call-done) | copy-start | bytes 12582916
  50.5 1.5 %copy-start.3 = (bf16[4096,128]{1,0:T(8,128)(2,1)S(1)}, bf16[4096,128]{1,0:T(8,128)(2,1)}, u32[]{:S(2)}) copy-start(bf16[4096,128]{1,0:T(8,128)(2,1)} %param.10) | copy-start | bytes 3145732
  52.0 3.2 %copy-start.2 = (bf16[4096,512]{1,0:T(8,128)(2,1)S(1)}, bf16[4096,512]{1,0:T(8,128)(2,1)}, u32[]{:S(2)}) copy-start(bf16[4096,512]{1,0:T(8,128)(2,1)} %param.9) | copy-start | bytes 12582916
  53.6 8.5 %collective-permute-start = (bf16[512,256]{0,1:T(8,128)(2,1)S(1)}, bf16[512,256]{0,1:T(8,128)(2,1)S(1)}, u32[]{:S(2)}, u32[]{:S(2)}) collective-permute-start(bf16[512,256]{0,1:T(8,128)(2,1)S(1)} %pad_maximum_fusion.1), channel_id=1, source_target_pairs={{0,8},{8,16},{16,24},{24,32},{32,40},{40,48},{48,56},{56,64},{64,7... | collective-permute-start | bytes 786440 | tf_op jit(solution)/shard_map/ppermute | solution.py:29
  66.8 21.0 %all-to-all-start = ((f32[32,5,128]{2,1,0:T(8,128)}), f32[32,5,128]{2,1,0:T(8,128)S(1)}, u32[]{:S(2)}, u32[]{:S(2)}) async-start(f32[32,5,128]{2,1,0:T(8,128)} %copy.102), calls=%async_computation | async-start | bytes 262144 | tf_op jit(solution)/shard_map/all_to_all | solution.py:60
Sparse Core Ops, SparseCore 0:
  9.8 37.1 all-gather.1
where the time goes:
time: 96.4 us; the launch traced here: 96.2 us
  waiting for transfers between devices  47.3 us (49%)
  between operations  14.4 us (15%)
  starting transfers between devices  13 us (13%)
  other arithmetic  9.3 us (10%)
  matrix products  9.06 us (9%)
  local copies, waits for them, and re-layouts  3.2 us (3%)
    all_gather x1, waiting for transfers between devices, shards(): lax.all_gather(tokens, 'proj', axis=1, tiled=True).astype(jnp.float32)  35.8 us
    all_to_all x1, starting transfers between devices, shards(): recv = lax.all_to_all(send, 'attn', split_axis=0, concat_axis=0, tiled=True)  11.3 us
    all_to_all x1, waiting for transfers between devices, shards(): recv = lax.all_to_all(send, 'attn', split_axis=0, concat_axis=0, tiled=True)  6.45 us
    dot_general x3, matrix products, shards(): jnp.dot(scaled, w, preferred_element_type=jnp.float32) * inverse  5.48 us
    ppermute x1, waiting for transfers between devices, shards(): lax.ppermute(kv, 'attn', [(i, (i + 1) % servers) for i in range(servers)])  4.36 us
    reduce_sum x1, other arithmetic, shards(): squares = jnp.sum(wide * wide, axis=1, keepdims=True)  3.23 us
    dot_general x4, matrix products, shards(): jnp.einsum('hqk,kd->hqd', w.astype(jnp.bfloat16), win[:, HEAD:], preferre...  2.09 us
  transfers between devices with their start and end apart: 3, of which 3 were waited for; matrix products, arithmetic and copies ran while one was open for 9% of the time, Pallas kernels for 0%

commit v1 on v0

--- a/solution.py
+++ b/solution.py
@@ -9,6 +9,13 @@
 norm_eps = 1e-05
 
 
+def all_by_exchange(shard, name, dim):
+    count = lax.axis_size(name)
+    parts = jnp.stack([shard for _ in range(count)])
+    parts = lax.all_to_all(parts, name, split_axis=0, concat_axis=0)
+    return jnp.concatenate(parts, axis=dim)
+
+
 def shards(tokens, norm_gain, w_query, w_key, value_matrix, doc_lengths, block_server):
     rows = tokens.shape[0]
     model_width = w_query.shape[0]
@@ -16,7 +23,7 @@
     blocks = rows // QB
     servers = lax.axis_size("attn")
     me = lax.axis_index("attn")
-    wide = lax.all_gather(tokens, "proj", axis=1, tiled=True).astype(jnp.float32)
+    wide = all_by_exchange(tokens, "proj", 1).astype(jnp.float32)
     scaled = (wide * norm_gain[None, :]).astype(jnp.bfloat16)
     squares = jnp.sum(wide * wide, axis=1, keepdims=True)
     inverse = lax.rsqrt(squares / model_width + norm_eps)

time: 96.4 us -> 103 us (1.068)
  between operations: 14.4 us -> 0.99 us
  waiting for transfers between devices: 47.3 us -> 58.1 us
  starting transfers between devices: 13 us -> 19.2 us
  local copies, waits for them, and re-layouts: 3.2 us -> 6.42 us
  matrix products: 9.06 us -> 7.6 us
  other arithmetic: 9.3 us -> 10.6 us
    all_to_all x0 -> x1, waiting for transfers between devices: none -> 48.3 us  [all_by_exchange(): parts = lax.all_to_all(parts, name, split_axis=0, concat_axis=0)]
    all_gather x1 -> x0, waiting for transfers between devices: 35.8 us -> none  [shards(): lax.all_gather(tokens, 'proj', axis=1, tiled=True).astype(jnp.float32)]
    all_to_all x0 -> x1, starting transfers between devices: none -> 4.68 us  [all_by_exchange(): parts = lax.all_to_all(parts, name, split_axis=0, concat_axis=0)]
    convert_element_type x0 -> x1, other arithmetic: none -> 2.71 us  [shards(): scaled = (wide * norm_gain[None, :]).astype(jnp.bfloat16)]
    another operation x1 -> x2, local copies, waits for them, and re-layouts: 0.76 us -> 2.44 us  [the longest x1 2.33 us: all_by_exchange(): parts = jnp.stack([shard for _ in range(count)])]
    unnamed x10 -> x13, local copies, waits for them, and re-layouts: 0.22 us -> 1.75 us
    dot_general x3, matrix products: 5.48 us -> 4.03 us  [shards(): jnp.dot(scaled, w, preferred_element_type=jnp.float32) * inverse]
    all_to_all x1, starting transfers between devices: 11.3 us -> 12.5 us  [shards(): recv = lax.all_to_all(send, 'attn', split_axis=0, concat_axis=0, tiled=True)]
  transfers between devices with their start and end apart: 3 -> 3, of which waited for: 3 -> 3; matrix products, arithmetic and copies ran while one was open for 9% -> 7% of each run, Pallas kernels for 0% -> 0%
where the time goes in v1:
time: 103 us
  waiting for transfers between devices  58.1 us (56%)
  starting transfers between devices  19.2 us (19%)
  other arithmetic  10.6 us (10%)
  matrix products  7.6 us (7%)
  local copies, waits for them, and re-layouts  6.42 us (6%)
    all_to_all x1, waiting for transfers between devices, all_by_exchange(): parts = lax.all_to_all(parts, name, split_axis=0, concat_axis=0)  48.3 us
    all_to_all x1, starting transfers between devices, shards(): recv = lax.all_to_all(send, 'attn', split_axis=0, concat_axis=0, tiled=True)  12.5 us
    all_to_all x1, waiting for transfers between devices, shards(): recv = lax.all_to_all(send, 'attn', split_axis=0, concat_axis=0, tiled=True)  6.45 us
    all_to_all x1, starting transfers between devices, all_by_exchange(): parts = lax.all_to_all(parts, name, split_axis=0, concat_axis=0)  4.68 us
    dot_general x3, matrix products, shards(): jnp.dot(scaled, w, preferred_element_type=jnp.float32) * inverse  4.03 us
    ppermute x1, waiting for transfers between devices, shards(): lax.ppermute(kv, 'attn', [(i, (i + 1) % servers) for i in range(servers)])  3.43 us
    reduce_sum x1, other arithmetic, shards(): squares = jnp.sum(wide * wide, axis=1, keepdims=True)  3.14 us
    convert_element_type x1, other arithmetic, shards(): scaled = (wide * norm_gain[None, :]).astype(jnp.bfloat16)  2.71 us
  transfers between devices with their start and end apart: 3, of which 3 were waited for; matrix products, arithmetic and copies ran while one was open for 7% of the time, Pallas kernels for 0%

profile of v1, /device:TPU:32, one launch (start us, length us, event | category | flops | bytes accessed | tf_op | source)
XLA Modules:
  0.0 102.9 jit_solution(13829106182458820553)
XLA Ops:
  0.6 1.3 %copy.89 = bf16[512,512]{0,1:T(8,128)(2,1)S(1)} copy(bf16[512,512]{1,0:T(8,128)(2,1)} %param.7) | data formatting | bytes 1048576 | tf_op args[0]
  2.0 2.3 %stack.4 = bf16[8,512,512]{1,2,0:T(8,128)(2,1)} broadcast(bf16[512,512]{0,1:T(8,128)(2,1)S(1)} %copy.89), dimensions={1,2} | broadcast | bytes 4718592 | tf_op jit(solution)/shard_map/stack | solution.py:14
  4.3 4.7 %all-to-all-start = ((bf16[8,512,512]{1,2,0:T(8,128)(2,1)}), bf16[8,512,512]{1,2,0:T(8,128)(2,1)}, u32[]{:S(2)}, u32[]{:S(2)}) async-start(bf16[8,512,512]{1,2,0:T(8,128)(2,1)} %stack.4), calls=%async_computation | async-start | bytes 8388608 | tf_op jit(solution)/shard_map/all_to_all | solution.py:15
  10.4 48.3 %all-to-all-done = bf16[8,512,512]{1,2,0:T(8,128)(2,1)} async-done(((bf16[8,512,512]{1,2,0:T(8,128)(2,1)}), bf16[8,512,512]{1,2,0:T(8,128)(2,1)}, u32[]{:S(2)}, u32[]{:S(2)}) %all-to-all-start) | async-done | bytes 4194336 | tf_op jit(solution)/shard_map/all_to_all | solution.py:15
  58.6 3.1 %multiply_reduce_fusion = f32[512]{0:T(512)S(1)} fusion(bf16[8,512,512]{1,2,0:T(8,128)(2,1)} %all-to-all-done), kind=kLoop, calls=%fused_computation.2 | loop fusion | flops 6290944 | bytes 4196352 | tf_op jit(solution)/shard_map/reduce_sum | solution.py:28
  61.8 2.7 %fusion = bf16[512,4096]{0,1:T(8,128)(2,1)S(1)} fusion(f32[4096]{0:T(1024)S(1)} %copy-done.1, bf16[8,512,512]{1,2,0:T(8,128)(2,1)} %all-to-all-done), kind=kLoop, calls=%fused_computation.1 | loop fusion | flops 6291456 | bytes 8404992 | tf_op jit(solution)/shard_map/convert_element_type | solution.py:27
  64.5 0.8 fusion.19
  65.4 0.4 copy-done.4
  65.8 0.8 fusion.18
  66.6 2.0 %collective-permute-start = (bf16[512,256]{0,1:T(8,128)(2,1)S(1)}, bf16[512,256]{0,1:T(8,128)(2,1)S(1)}, u32[]{:S(2)}, u32[]{:S(2)}) collective-permute-start(bf16[512,256]{0,1:T(8,128)(2,1)S(1)} %pad_maximum_fusion.1), channel_id=1, source_target_pairs={{0,8},{8,16},{16,24},{24,32},{32,40},{40,48},{48,56},{56,64},{64,7... | collective-permute-start | bytes 786440 | tf_op jit(solution)/shard_map/ppermute | solution.py:36
  68.6 2.4 %fusion.9 = bf16[512,512]{0,1:T(8,128)(2,1)S(1)} fusion(bf16[512,4096]{0,1:T(8,128)(2,1)S(1)} %fusion, bf16[4096,512]{1,0:T(8,128)(2,1)S(1)} %copy-done.3, f32[512]{0:T(512)S(1)} %add_rsqrt_fusion), kind=kOutput, calls=%fused_computation.20 | convolution fusion | flops 2148007936 | bytes 8914944 | tf_op jit(solution)/shard_map/dot_general | solution.py:30
  71.1 3.4 %collective-permute-done = bf16[512,256]{0,1:T(8,128)(2,1)S(1)} collective-permute-done((bf16[512,256]{0,1:T(8,128)(2,1)S(1)}, bf16[512,256]{0,1:T(8,128)(2,1)S(1)}, u32[]{:S(2)}, u32[]{:S(2)}) %collective-permute-start) | collective-permute-done | bytes 262176 | tf_op jit(solution)/shard_map/ppermute | solution.py:36
  74.6 0.4 fusion.51
  75.6 0.4 fusion.52
  76.6 0.4 fusion.53
  77.6 0.4 fusion.54
  78.5 0.7 copy.106
  79.1 12.5 %all-to-all-start.1 = ((f32[32,5,128]{2,1,0:T(8,128)}), f32[32,5,128]{2,1,0:T(8,128)S(1)}, u32[]{:S(2)}, u32[]{:S(2)}) async-start(f32[32,5,128]{2,1,0:T(8,128)} %copy.106), calls=%async_computation.1 | async-start | bytes 262144 | tf_op jit(solution)/shard_map/all_to_all | solution.py:67
  91.6 1.0 fusion.14
  93.0 1.0 copy.102
  94.0 0.8 pad_maximum_fusion
  94.9 6.4 %all-to-all-done.1 = f32[32,5,128]{2,1,0:T(8,128)S(1)} async-done(((f32[32,5,128]{2,1,0:T(8,128)}), f32[32,5,128]{2,1,0:T(8,128)S(1)}, u32[]{:S(2)}, u32[]{:S(2)}) %all-to-all-start.1) | async-done | bytes 81952 | tf_op jit(solution)/shard_map/all_to_all | solution.py:67
  101.3 0.7 compare_reduce_fusion
  102.2 0.7 select_reduce_fusion
  (55 shorter events, 4.3 us)
Async XLA Ops:
  0.6 63.9 %copy-start = (bf16[4096,128]{1,0:T(8,128)(2,1)S(1)}, bf16[4096,128]{1,0:T(8,128)(2,1)}, u32[]{:S(2)}) copy-start(bf16[4096,128]{1,0:T(8,128)(2,1)} %param.11) | copy-start | bytes 3145732
  4.3 4.7 %copy-start.2 = (s32[128]{0:T(128)S(1)}, s32[128]{0:T(128)}, u32[]{:S(2)}) copy-start(s32[128]{0:T(128)} %param.12) | copy-start | bytes 1540
  4.3 5.1 %copy-start.5 = (s32[4]{0:T(128)S(1)}, s32[4]{0:T(128)}, u32[]{:S(2)}) copy-start(s32[4]{0:T(128)} %param.13) | copy-start | bytes 52
  4.3 54.3 %all-to-all-start = ((bf16[8,512,512]{1,2,0:T(8,128)(2,1)}), bf16[8,512,512]{1,2,0:T(8,128)(2,1)}, u32[]{:S(2)}, u32[]{:S(2)}) async-start(bf16[8,512,512]{1,2,0:T(8,128)(2,1)} %stack.4), calls=%async_computation | async-start | bytes 8388608 | tf_op jit(solution)/shard_map/all_to_all | solution.py:15
  10.4 51.4 %copy-start.1 = (f32[4096]{0:T(1024)S(1)}, f32[4096]{0:T(1024)}, u32[]{:S(2)}) copy-start(f32[4096]{0:T(1024)} %param.8) | copy-start | bytes 49156
  64.5 1.2 %copy-start.4 = (bf16[4096,128]{1,0:T(8,128)(2,1)S(1)}, bf16[4096,128]{1,0:T(8,128)(2,1)}, u32[]{:S(2)}) copy-start(bf16[4096,128]{1,0:T(8,128)(2,1)} %param.10) | copy-start | bytes 3145732
  65.8 2.9 %copy-start.3 = (bf16[4096,512]{1,0:T(8,128)(2,1)S(1)}, bf16[4096,512]{1,0:T(8,128)(2,1)}, u32[]{:S(2)}) copy-start(bf16[4096,512]{1,0:T(8,128)(2,1)} %param.9) | copy-start | bytes 12582916
  66.6 7.9 %collective-permute-start = (bf16[512,256]{0,1:T(8,128)(2,1)S(1)}, bf16[512,256]{0,1:T(8,128)(2,1)S(1)}, u32[]{:S(2)}, u32[]{:S(2)}) collective-permute-start(bf16[512,256]{0,1:T(8,128)(2,1)S(1)} %pad_maximum_fusion.1), channel_id=1, source_target_pairs={{0,8},{8,16},{16,24},{24,32},{32,40},{40,48},{48,56},{56,64},{64,7... | collective-permute-start | bytes 786440 | tf_op jit(solution)/shard_map/ppermute | solution.py:36
  79.1 22.2 %all-to-all-start.1 = ((f32[32,5,128]{2,1,0:T(8,128)}), f32[32,5,128]{2,1,0:T(8,128)S(1)}, u32[]{:S(2)}, u32[]{:S(2)}) async-start(f32[32,5,128]{2,1,0:T(8,128)} %copy.106), calls=%async_computation.1 | async-start | bytes 262144 | tf_op jit(solution)/shard_map/all_to_all | solution.py:67
